TPU v7x, 256 devices: a whole 4x4x8 slice. The times are simulated.
256 devices in a mesh: group: 2 (over core), ctx: 32 (over x, z_hi, y), tp: 4 (over z_lo).
Axes of the slice: x: 4, y: 4, z: 8 (z_hi: 2, z_lo: 4; z = z_hi * 4 + z_lo), core: 2. Of those that a mesh axis runs over, the one named last changes fastest.
Arguments:
- activations: bfloat16 [8192, 8192], P(('group', 'ctx')), may hold values from -6 to 6
- queries: bfloat16 [8192, 4096], P(('group', 'ctx'), 'tp'), may hold values from -400 to 400
- out_grad: bfloat16 [8192, 4096], P(('group', 'ctx'), 'tp'), may hold values from -6 to 6
- key_weight: bfloat16 [8192, 512], P('ctx', 'tp'), may hold values from -0.0625 to 0.0625
- value_weight: bfloat16 [8192, 512], P('ctx', 'tp'), may hold values from -0.0625 to 0.0625
- sessions: int32 [32, 128], P('ctx'), may hold values from 0 to 3, never falling along the last dimension, each value on 1 to 64 neighbouring positions
Outputs:
- attention: bfloat16 [8192, 4096], P(('group', 'ctx'), 'tp')
- query_grad: bfloat16 [8192, 4096], P(('group', 'ctx'), 'tp')
- key_weight_grad: float32 [8192, 512], P(('group', 'ctx'), 'tp')
- value_weight_grad: float32 [8192, 512], P(('group', 'ctx'), 'tp')
- input_grad: bfloat16 [8192, 8192], P(('group', 'ctx'), 'tp')
Inputs may be any that keep to these rules, and one draw needn't show every extreme that they name: `sessions`: each row never falls; every session in a row has 1 to 64 tokens, and one session of each row has exactly that many.
All inputs are finite; a program needn't handle non-finite values.
Results may differ from a plain program's by a relative error of at most 0.025.
The roundings to bfloat16 on the way count: a program that leaves them out, or rounds other values in their place, can miss the bound.
Values may be sent and summed in bfloat16 or wider, within the bound.
No kernel may reach another device: no remote copies, remote signals or barrier semaphores. Data moves between devices by JAX's collectives and lax.ppermute only.
A program may use at most 64 MiB of HBM per device.

v0:
```python
import math
import jax
import jax.numpy as jnp
from jax import lax
from jax.sharding import PartitionSpec as P

HQ = 32
KVH = 4
HD = 128
THETA = 500000.0


def cut_along(array, dim, count):
    before, after = (array.shape[:dim], array.shape[dim + 1 :])
    return jnp.moveaxis(array.reshape(*before, count, -1, *after), dim, 0)


def sum_at_owner(array, axis, dim):
    blocks = cut_along(array, dim, lax.axis_size(axis))
    arrived = lax.all_to_all(blocks, axis, split_axis=0, concat_axis=0, tiled=True)
    return arrived.sum(axis=0)


def rotate(vector, positions, turn_sign):
    half_dim = HD // 2
    frequency = THETA ** (-2.0 * jnp.arange(half_dim, dtype=jnp.float32) / HD)
    angles = positions.astype(jnp.float32)[:, None] * frequency[None, :]
    cosine = jnp.cos(angles)[:, None, :]
    sine_table = turn_sign * jnp.sin(angles)[:, None, :]
    shaped = vector.reshape(vector.shape[0], -1, HD)
    first_half = shaped[..., :half_dim]
    second_half = shaped[..., half_dim:]
    turned = jnp.concatenate(
        [
            first_half * cosine - second_half * sine_table,
            second_half * cosine + first_half * sine_table,
        ],
        -1,
    )
    return turned.reshape(vector.shape)


def body(activations, queries, out_grad, key_weight, value_weight, sessions):
    score_scale = 1.0 / math.sqrt(HD)
    tok_rows = activations.shape[0]
    ctx_count = lax.axis_size("ctx")
    total_rows = ctx_count * tok_rows
    key_block = min(total_rows, tok_rows * max(1, 512 // tok_rows))
    is_long = lax.axis_index("group") == 0
    own_first = lax.axis_index("ctx") * tok_rows
    local_rows = jnp.arange(tok_rows, dtype=jnp.int32)
    query_rows = own_first + local_rows
    positions = jnp.where(is_long, query_rows, local_rows)
    own_sessions = sessions[0]
    kv_cols = key_weight.shape[1]
    kv_heads = kv_cols // HD
    group_heads = HQ // KVH
    both_weights = jnp.concatenate([key_weight, value_weight], 1)
    whole_weights = lax.all_gather(both_weights, "ctx", axis=0, tiled=True)
    projected = jnp.dot(activations, whole_weights, preferred_element_type=jnp.float32)
    rotated_keys = rotate(projected[:, :kv_cols], positions, 1.0).astype(jnp.bfloat16)
    value_rows = projected[:, kv_cols:].astype(jnp.bfloat16)
    rotated = rotate(queries.astype(jnp.float32), positions, 1.0).astype(jnp.bfloat16)
    query_heads = rotated.reshape(tok_rows, kv_heads, group_heads, HD)
    grad_heads = out_grad.reshape(tok_rows, kv_heads, group_heads, HD)
    context = lax.all_gather(
        jnp.concatenate([rotated_keys, value_rows], 1), "ctx", axis=0, tiled=True
    )
    first_block = jnp.where(is_long, 0, own_first // key_block)
    stop_block = own_first // key_block + 1

    def block_scores(block_index):
        block_first = (block_index * key_block).astype(jnp.int32)
        block_kv = lax.dynamic_slice_in_dim(context, block_first, key_block, 0)
        block_keys = block_kv[:, :kv_cols].reshape(key_block, kv_heads, HD)
        block_values = block_kv[:, kv_cols:].reshape(key_block, kv_heads, HD)
        key_rows = block_first + jnp.arange(key_block, dtype=jnp.int32)
        key_sessions = lax.dynamic_update_slice(
            jnp.full((key_block,), -1, jnp.int32), own_sessions, (own_first - block_first,)
        )
        same_session = own_sessions[:, None] == key_sessions[None, :]
        allowed = (key_rows[None, :] <= query_rows[:, None]) & (is_long | same_session)
        scores = (
            jnp.einsum(
                "qkgd,skd->kgqs", query_heads, block_keys, preferred_element_type=jnp.float32
            )
            * score_scale
        )
        scores = jnp.where(allowed[None, None], scores, -jnp.inf)
        return (scores, block_keys, block_values, block_first)

    def max_pass(block_index, loop_state):
        running_max, running_sum = loop_state
        scores = block_scores(block_index)[0]
        new_max = jnp.maximum(running_max, jnp.max(scores, -1))
        running_sum = running_sum * jnp.exp(running_max - new_max) + jnp.sum(
            jnp.exp(scores - new_max[..., None]), -1
        )
        return (new_max, running_sum)

    stat_shape = (kv_heads, group_heads, tok_rows)
    row_max, row_total = lax.fori_loop(
        first_block,
        stop_block,
        max_pass,
        (jnp.full(stat_shape, -jnp.inf, jnp.float32), jnp.zeros(stat_shape, jnp.float32)),
    )
    log_total = row_max + jnp.log(row_total)

    def output_pass(block_index, running):
        scores, block_keys, block_values, block_first = block_scores(block_index)
        rounded_weights = jnp.exp(scores - log_total[..., None]).astype(jnp.bfloat16)
        return running + jnp.einsum(
            "kgqs,skd->qkgd", rounded_weights, block_values, preferred_element_type=jnp.float32
        )

    attended = lax.fori_loop(
        first_block,
        stop_block,
        output_pass,
        jnp.zeros((tok_rows, kv_heads, group_heads, HD), jnp.float32),
    )
    attention = attended.reshape(tok_rows, kv_heads * group_heads * HD).astype(jnp.bfloat16)
    out_dot = jnp.einsum(
        "qkgd,qkgd->kgq",
        grad_heads.astype(jnp.float32),
        attention.astype(jnp.float32).reshape(tok_rows, kv_heads, group_heads, HD),
    )

    def grad_pass(block_index, loop_state):
        query_acc, key_buffer = loop_state
        scores, block_keys, block_values, block_first = block_scores(block_index)
        weights = jnp.exp(scores - log_total[..., None])
        rounded_weights = weights.astype(jnp.bfloat16)
        prob_grad = jnp.einsum(
            "qkgd,skd->kgqs", grad_heads, block_values, preferred_element_type=jnp.float32
        )
        score_grad = (weights * (prob_grad - out_dot[..., None])).astype(jnp.bfloat16)
        query_acc = query_acc + jnp.einsum(
            "kgqs,skd->qkgd", score_grad, block_keys, preferred_element_type=jnp.float32
        )
        key_part = (
            jnp.einsum(
                "kgqs,qkgd->skd", score_grad, query_heads, preferred_element_type=jnp.float32
            )
            * score_scale
        )
        value_part = jnp.einsum(
            "kgqs,qkgd->skd", rounded_weights, grad_heads, preferred_element_type=jnp.float32
        )
        update = jnp.concatenate(
            [key_part.reshape(key_block, kv_cols), value_part.reshape(key_block, kv_cols)], 1
        )
        key_buffer = lax.dynamic_update_slice(key_buffer, update, (block_first, jnp.int32(0)))
        return (query_acc, key_buffer)

    query_acc, key_buffer = lax.fori_loop(
        first_block,
        stop_block,
        grad_pass,
        (
            jnp.zeros((tok_rows, kv_heads, group_heads, HD), jnp.float32),
            jnp.zeros((total_rows, 2 * kv_cols), jnp.float32),
        ),
    )
    query_grad = rotate(
        query_acc.reshape(tok_rows, kv_heads * group_heads * HD) * score_scale, positions, -1.0
    ).astype(jnp.bfloat16)
    summed = lax.psum_scatter(key_buffer, "ctx", scatter_dimension=0, tiled=True)
    key_grad = rotate(summed[:, :kv_cols], positions, -1.0).astype(jnp.bfloat16)
    value_grad = summed[:, kv_cols:].astype(jnp.bfloat16)
    kv_grads = jnp.concatenate([key_grad, value_grad], 1)
    input_terms = lax.dot_general(
        kv_grads, whole_weights, (((1,), (1,)), ((), ())), preferred_element_type=jnp.float32
    )
    input_grad = sum_at_owner(input_terms, "tp", 1).astype(jnp.bfloat16)
    column_rows = lax.all_to_all(
        activations, ("group", "ctx"), split_axis=1, concat_axis=0, tiled=True
    )
    owned_rows = lax.dot_general(
        column_rows,
        lax.all_gather(kv_grads, ("group", "ctx"), axis=0, tiled=True),
        (((0,), (0,)), ((), ())),
        preferred_element_type=jnp.float32,
    )
    key_weight_grad = owned_rows[:, :kv_cols]
    value_weight_grad = owned_rows[:, kv_cols:]
    return (attention, query_grad, key_weight_grad, value_weight_grad, input_grad)


def solution(mesh):
    placed = (
        P(("group", "ctx"), None),
        P(("group", "ctx"), "tp"),
        P(("group", "ctx"), "tp"),
        P("ctx", "tp"),
        P("ctx", "tp"),
        P("ctx", None),
    )
    return jax.shard_map(
        body,
        mesh=mesh,
        in_specs=placed,
        out_specs=(
            P(("group", "ctx"), "tp"),
            P(("group", "ctx"), "tp"),
            P(("group", "ctx"), "tp"),
            P(("group", "ctx"), "tp"),
            P(("group", "ctx"), "tp"),
        ),
        check_vma=False,
    )
```

profile of v0, /device:TPU:8, one launch (start us, length us, event | category | flops | bytes accessed | tf_op | source)
XLA Modules:
  0.0 707.3 jit_solution(11987555391099404159)
XLA Ops:
  7.2 1.5 pad_maximum_fusion.2
  8.9 116.2 %all-gather.4.cloned.1.call-done = bf16[8192,256]{1,0:T(8,128)(2,1)} async-done(((bf16[256,256]{1,0:T(8,128)(2,1)}), bf16[8192,256]{1,0:T(8,128)(2,1)}) %all-gather.4.cloned.1.call-update) | async-done | bytes 4194320 | tf_op jit(solution)/shard_map/all_gather | solution.py:59
  125.1 4.1 convolution_bitcast_fusion.5
  129.5 0.6 pad_maximum_fusion.3
  131.1 0.8 copy.112
  131.9 91.5 %all-gather.6.cloned.1.call-done = bf16[4096,256]{0,1:T(8,128)(2,1)} async-done(((bf16[128,256]{0,1:T(8,128)(2,1)}), bf16[4096,256]{0,1:T(8,128)(2,1)}) %all-gather.6.cloned.1.call-update) | async-done | bytes 2097168 | tf_op jit(solution)/shard_map/all_gather | solution.py:66
  223.4 3.3 copy.81
  226.7 1.5 while.40
  226.8 0.2 dynamic_update_slice.65
  227.0 0.2 or_and_fusion.6
  227.2 0.4 fusion.83
  227.7 0.4 exponential_reduce_fusion.2
  228.2 0.6 log_add_fusion
  228.8 2.0 while.41
  228.9 0.2 dynamic_update_slice.67
  229.1 0.2 or_and_fusion.7
  229.3 1.5 fusion.85
  230.9 1.0 bitcast_convert_fusion
  231.8 1.4 copy.105
  233.2 0.2 multiply_reduce_fusion
  233.5 2.5 broadcast_in_dim.52
  236.0 6.4 while.42
  236.0 0.2 dynamic_update_slice.70
  236.5 1.5 fusion.93
  237.9 1.3 fusion.94
  239.3 1.3 fusion.95
  240.6 0.5 convolution_bitcast_fusion.7
  241.0 0.5 fusion.96
  241.5 0.9 maximum_dynamic-update-slice_fusion.2
  242.4 1.6 copy-done
  244.0 2.5 copy.87
  246.5 70.4 %all-to-all-start = ((bf16[128,64,128]{0,2,1:T(8,128)(2,1)}), bf16[128,64,128]{0,2,1:T(8,128)(2,1)S(1)}, u32[]{:S(2)}, u32[]{:S(2)}) async-start(bf16[128,64,128]{0,2,1:T(8,128)(2,1)} %bitcast.241), calls=%async_computation.1 | async-start | bytes 4194304 | tf_op jit(solution)/shard_map/all_to_all | solution.py:177
  317.0 260.9 %reduce-scatter.2.cloned.1.call-done = f32[128,256]{0,1:T(8,128)} async-done(((f32[4096,256]{0,1:T(8,128)}), f32[128,256]{0,1:T(8,128)}) %reduce-scatter.2.cloned.1.call-update) | async-done | bytes 131088 | tf_op jit(solution)/shard_map/reduce_scatter | solution.py:169
  577.9 0.8 slice.125
  578.8 0.8 slice_bitcast_fusion
  579.9 0.6 pad_maximum_fusion.4
  580.5 3.7 fusion.60
  584.2 2.2 copy.114
  586.4 1.3 copy-done.1
  587.7 5.1 all-to-all-start.1
  592.9 3.3 copy.88
  596.2 0.8 copy.107
  597.2 0.8 copy.108
  598.0 94.4 %all-to-all-done.1 = f32[4,128,2048]{2,1,0:T(8,128)} async-done(((f32[4,128,2048]{2,1,0:T(8,128)}), f32[4,128,2048]{2,1,0:T(8,128)}, u32[]{:S(2)}, u32[]{:S(2)}) %all-to-all-start.1) | async-done | bytes 4194336 | tf_op jit(solution)/shard_map/all_to_all | solution.py:20
  692.4 3.4 reduce_sum.20
  695.9 3.4 convolution_bitcast_fusion.4
  699.3 0.7 copy.90
  700.1 0.7 copy.91
  (64 shorter events, 2.0 us)
Async XLA Ops:
  7.2 117.9 %all-gather.4.cloned.1.call-start = ((), (), s32[]{:S(2)}) async-start(), calls=%async_computation.3 | async-start | bytes 4325376 | tf_op jit(solution)/shard_map/all_gather | solution.py:59
  8.8 214.6 %all-gather.6.cloned.1.call-start = ((), (), s32[]{:S(2)}) async-start(), calls=%async_computation.4 | async-start | bytes 2162688 | tf_op jit(solution)/shard_map/all_gather | solution.py:66
  8.9 121.5 %copy-start.8 = (f32[128]{0:T(128)}, f32[128]{0:T(128)S(1)}, u32[]{:S(2)}) copy-start(f32[128]{0:T(128)S(1)} %fusion.59) | copy-start | bytes 1540
  8.9 121.4 %copy-start.6 = (bf16[128,1024]{1,0:T(8,128)(2,1)S(1)}, bf16[128,1024]{1,0:T(8,128)(2,1)}, u32[]{:S(2)}) copy-start(bf16[128,1024]{1,0:T(8,128)(2,1)} %param.13) | copy-start | bytes 786436
  129.3 1.6 copy-start.4
  130.2 447.8 %reduce-scatter.2.cloned.1.call-start = ((), (), s32[]{:S(2)}) async-start(), calls=%async_computation.5 | async-start | bytes 4325376 | tf_op jit(solution)/shard_map/reduce_scatter | solution.py:169
  131.9 94.8 %copy-start.7 = (s32[1,128]{1,0:T(1,128)S(1)}, s32[1,128]{1,0:T(1,128)}, u32[]{:S(2)}) copy-start(s32[1,128]{1,0:T(1,128)} %param.17) | copy-start | bytes 1540
  230.9 2.6 copy-start.2
  230.9 2.3 copy-start.5
  242.4 1.6 copy-start
  246.5 333.1 %copy-start.9 = (f32[128]{0:T(128)S(1)}, f32[128]{0:T(128)}, u32[]{:S(2)}) copy-start(f32[128]{0:T(128)} %copy-done.8) | copy-start | bytes 1540
  246.5 339.9 %all-to-all-start = ((bf16[128,64,128]{0,2,1:T(8,128)(2,1)}), bf16[128,64,128]{0,2,1:T(8,128)(2,1)S(1)}, u32[]{:S(2)}, u32[]{:S(2)}) async-start(bf16[128,64,128]{0,2,1:T(8,128)(2,1)} %bitcast.241), calls=%async_computation.1 | async-start | bytes 4194304 | tf_op jit(solution)/shard_map/all_to_all | solution.py:177
  317.0 378.9 %all-gather.8.cloned.1.call-start = ((), (), s32[]{:S(2)}) async-start(), calls=%async_computation.6 | async-start | bytes 4259840 | tf_op jit(solution)/shard_map/all_gather | solution.py:182
  586.4 1.3 copy-start.1
  587.7 104.7 %all-to-all-start.1 = ((f32[4,128,2048]{2,1,0:T(8,128)}), f32[4,128,2048]{2,1,0:T(8,128)}, u32[]{:S(2)}, u32[]{:S(2)}) async-start(f32[4,128,2048]{2,1,0:T(8,128)} %bitcast.237), calls=%async_computation.2 | async-start | bytes 8388608 | tf_op jit(solution)/shard_map/all_to_all | solution.py:20
  592.9 3.3 copy-start.3
Sparse Core Ops, SparseCore 0:
  12.1 113.0 all-gather.3
  130.3 93.0 all-gather.5
  242.6 335.3 reduce-scatter.1
  581.7 100.2 all-gather.7
where the time goes:
time: 709 us; the launch traced here: 707 us
  waiting for transfers between devices  563 us (79%)
  starting transfers between devices  75.7 us (11%)
  local copies, waits for them, and re-layouts  25 us (4%)
  matrix products  18.2 us (3%)
  between operations  14.1 us (2%)
  other arithmetic  10.9 us (2%)
    reduce_scatter x1, waiting for transfers between devices, body(): lax.psum_scatter(key_buffer, 'ctx', scatter_dimension=0, tiled=True)  261 us
    all_gather x1, waiting for transfers between devices, body(): whole_weights = lax.all_gather(both_weights, 'ctx', axis=0, tiled=True)  116 us
    all_to_all x1, waiting for transfers between devices, sum_at_owner(): lax.all_to_all(blocks, axis, split_axis=0, concat_axis=0, tiled=True)  94.4 us
    all_gather x1, waiting for transfers between devices, body(): lax.all_gather(jnp.concatenate([rotated_keys, value_rows], 1), 'ctx', axi...  91.5 us
    all_to_all x1, starting transfers between devices, body(): lax.all_to_all(activations, ('group', 'ctx'), split_axis=1, concat_axis=0...  70.4 us
  transfers between devices with their start and end apart: 6, of which 4 were waited for; matrix products, arithmetic and copies ran while one was open for 3% of the time, Pallas kernels for 0%

commit v1 on v0

--- a/solution.py
+++ b/solution.py
@@ -63,8 +63,14 @@
     rotated = rotate(queries.astype(jnp.float32), positions, 1.0).astype(jnp.bfloat16)
     query_heads = rotated.reshape(tok_rows, kv_heads, group_heads, HD)
     grad_heads = out_grad.reshape(tok_rows, kv_heads, group_heads, HD)
-    context = lax.all_gather(
-        jnp.concatenate([rotated_keys, value_rows], 1), "ctx", axis=0, tiled=True
+    context = jnp.concatenate(
+        lax.all_to_all(
+            jnp.stack([jnp.concatenate([rotated_keys, value_rows], 1)] * lax.axis_size("ctx")),
+            "ctx",
+            0,
+            0,
+        ),
+        axis=0,
     )
     first_block = jnp.where(is_long, 0, own_first // key_block)
     stop_block = own_first // key_block + 1

time: 709 us -> 668 us (0.942)
  waiting for transfers between devices: 563 us -> 494 us
  starting transfers between devices: 75.7 us -> 105 us
    all_gather x1 -> x0, waiting for transfers between devices: 91.5 us -> none  [body(): lax.all_gather(jnp.concatenate([rotated_keys, value_rows], 1), 'ctx', axi...]
    all_to_all x0 -> x1, waiting for transfers between devices: none -> 24.5 us  [body(): lax.all_to_all(jnp.stack([jnp.concatenate([rotated_keys, value_rows], 1)]...]
    all_to_all x1, starting transfers between devices: 5.11 us -> 23.4 us  [sum_at_owner(): lax.all_to_all(blocks, axis, split_axis=0, concat_axis=0, tiled=True)]
where the time goes in v1:
time: 668 us; the launch traced here: 665 us
  waiting for transfers between devices  494 us (74%)
  starting transfers between devices  105 us (16%)
  local copies, waits for them, and re-layouts  23.6 us (4%)
  matrix products  18.3 us (3%)
  between operations  14.1 us (2%)
  other arithmetic  10.2 us (2%)
    reduce_scatter x1, waiting for transfers between devices, body(): lax.psum_scatter(key_buffer, 'ctx', scatter_dimension=0, tiled=True)  262 us
    all_gather x1, waiting for transfers between devices, body(): whole_weights = lax.all_gather(both_weights, 'ctx', axis=0, tiled=True)  116 us
    all_to_all x1, waiting for transfers between devices, sum_at_owner(): lax.all_to_all(blocks, axis, split_axis=0, concat_axis=0, tiled=True)  91.8 us
    all_to_all x1, starting transfers between devices, body(): lax.all_to_all(activations, ('group', 'ctx'), split_axis=1, concat_axis=0...  74.8 us
    all_to_all x1, waiting for transfers between devices, body(): lax.all_to_all(jnp.stack([jnp.concatenate([rotated_keys, value_rows], 1)]...  24.5 us
    all_to_all x1, starting transfers between devices, sum_at_owner(): lax.all_to_all(blocks, axis, split_axis=0, concat_axis=0, tiled=True)  23.4 us
  transfers between devices with their start and end apart: 6, of which 4 were waited for; matrix products, arithmetic and copies ran while one was open for 3% of the time, Pallas kernels for 0%

profile of v1, /device:TPU:8, one launch (start us, length us, event | category | flops | bytes accessed | tf_op | source)
XLA Modules:
  0.0 665.4 jit_solution(16815579231978557974)
XLA Ops:
  7.2 1.5 pad_maximum_fusion.2
  8.8 116.3 %all-gather.3.cloned.1.call-done = bf16[8192,256]{1,0:T(8,128)(2,1)} async-done(((bf16[256,256]{1,0:T(8,128)(2,1)}), bf16[8192,256]{1,0:T(8,128)(2,1)}) %all-gather.3.cloned.1.call-update) | async-done | bytes 4194320 | tf_op jit(solution)/shard_map/all_gather | solution.py:59
  125.1 4.1 convolution_bitcast_fusion.5
  129.6 1.6 stack.2
  131.2 6.3 all-to-all-start
  138.7 0.8 copy.104
  139.4 24.5 %all-to-all-done = bf16[32,128,256]{2,1,0:T(8,128)(2,1)S(1)} async-done(((bf16[32,128,256]{2,1,0:T(8,128)(2,1)}), bf16[32,128,256]{2,1,0:T(8,128)(2,1)S(1)}, u32[]{:S(2)}, u32[]{:S(2)}) %all-to-all-start) | async-done | bytes 2097184 | tf_op jit(solution)/shard_map/all_to_all | solution.py:67
  163.9 1.4 while.40
  164.0 0.2 dynamic_update_slice.65
  164.2 0.2 or_and_fusion.6
  164.4 0.4 fusion.83
  164.9 0.4 exponential_reduce_fusion.2
  165.4 0.6 log_add_fusion
  166.0 2.0 while.41
  166.1 0.2 dynamic_update_slice.67
  166.6 1.5 fusion.85
  168.1 1.0 bitcast_convert_fusion
  169.1 1.4 copy.97
  170.4 0.2 multiply_reduce_fusion
  170.8 2.5 broadcast_in_dim.52
  173.2 6.3 while.42
  173.2 0.2 dynamic_update_slice.70
  173.5 0.2 or_and_fusion.8
  173.7 1.5 fusion.93
  175.2 1.3 fusion.94
  176.5 1.3 fusion.95
  177.8 0.5 convolution_bitcast_fusion.7
  178.2 0.5 fusion.96
  178.7 0.9 maximum_dynamic-update-slice_fusion.2
  179.6 1.6 copy-done
  181.2 2.5 copy.79
  183.7 74.8 %all-to-all-start.1 = ((bf16[128,64,128]{0,2,1:T(8,128)(2,1)}), bf16[128,64,128]{0,2,1:T(8,128)(2,1)S(1)}, u32[]{:S(2)}, u32[]{:S(2)}) async-start(bf16[128,64,128]{0,2,1:T(8,128)(2,1)} %bitcast.242), calls=%async_computation.2 | async-start | bytes 4194304 | tf_op jit(solution)/shard_map/all_to_all | solution.py:183
  258.6 261.6 %reduce-scatter.2.cloned.1.call-done = f32[128,256]{0,1:T(8,128)} async-done(((f32[4096,256]{0,1:T(8,128)}), f32[128,256]{0,1:T(8,128)}) %reduce-scatter.2.cloned.1.call-update) | async-done | bytes 131088 | tf_op jit(solution)/shard_map/reduce_scatter | solution.py:175
  520.2 0.8 slice.125
  521.0 0.8 slice_bitcast_fusion
  522.1 0.6 pad_maximum_fusion.4
  522.8 3.7 fusion.60
  526.4 2.2 copy.106
  528.7 1.3 copy-done.1
  530.0 23.4 %all-to-all-start.2 = ((f32[4,128,2048]{2,1,0:T(8,128)}), f32[4,128,2048]{2,1,0:T(8,128)}, u32[]{:S(2)}, u32[]{:S(2)}) async-start(f32[4,128,2048]{2,1,0:T(8,128)} %bitcast.238), calls=%async_computation.3 | async-start | bytes 8388608 | tf_op jit(solution)/shard_map/all_to_all | solution.py:20
  553.4 3.3 copy.80
  556.7 0.9 copy.99
  557.7 0.9 copy.100
  558.6 91.8 %all-to-all-done.2 = f32[4,128,2048]{2,1,0:T(8,128)} async-done(((f32[4,128,2048]{2,1,0:T(8,128)}), f32[4,128,2048]{2,1,0:T(8,128)}, u32[]{:S(2)}, u32[]{:S(2)}) %all-to-all-start.2) | async-done | bytes 4194336 | tf_op jit(solution)/shard_map/all_to_all | solution.py:20
  650.4 3.4 reduce_sum.20
  653.9 3.5 convolution_bitcast_fusion.4
  657.4 0.7 copy.82
  658.1 0.7 copy.83
  (64 shorter events, 2.3 us)
Async XLA Ops:
  7.2 117.9 %all-gather.3.cloned.1.call-start = ((), (), s32[]{:S(2)}) async-start(), calls=%async_computation.4 | async-start | bytes 4325376 | tf_op jit(solution)/shard_map/all_gather | solution.py:59
  8.8 129.0 %copy-start.8 = (f32[128]{0:T(128)}, f32[128]{0:T(128)S(1)}, u32[]{:S(2)}) copy-start(f32[128]{0:T(128)S(1)} %fusion.59) | copy-start | bytes 1540
  131.2 6.4 copy-start.6
  131.2 32.7 %all-to-all-start = ((bf16[32,128,256]{2,1,0:T(8,128)(2,1)}), bf16[32,128,256]{2,1,0:T(8,128)(2,1)S(1)}, u32[]{:S(2)}, u32[]{:S(2)}) async-start(bf16[32,128,256]{2,1,0:T(8,128)(2,1)} %stack.2), calls=%async_computation | async-start | bytes 4194304 | tf_op jit(solution)/shard_map/all_to_all | solution.py:67
  137.6 1.0 copy-start.4
  137.6 26.4 %copy-start.7 = (s32[1,128]{1,0:T(1,128)S(1)}, s32[1,128]{1,0:T(1,128)}, u32[]{:S(2)}) copy-start(s32[1,128]{1,0:T(1,128)} %param.17) | copy-start | bytes 1540
  137.6 382.6 %reduce-scatter.2.cloned.1.call-start = ((), (), s32[]{:S(2)}) async-start(), calls=%async_computation.5 | async-start | bytes 4325376 | tf_op jit(solution)/shard_map/reduce_scatter | solution.py:175
  168.1 2.6 copy-start.2
  168.1 2.3 copy-start.5
  179.6 1.6 copy-start
  183.7 338.2 %copy-start.9 = (f32[128]{0:T(128)S(1)}, f32[128]{0:T(128)}, u32[]{:S(2)}) copy-start(f32[128]{0:T(128)} %copy-done.8) | copy-start | bytes 1540
  183.7 345.0 %all-to-all-start.1 = ((bf16[128,64,128]{0,2,1:T(8,128)(2,1)}), bf16[128,64,128]{0,2,1:T(8,128)(2,1)S(1)}, u32[]{:S(2)}, u32[]{:S(2)}) async-start(bf16[128,64,128]{0,2,1:T(8,128)(2,1)} %bitcast.242), calls=%async_computation.2 | async-start | bytes 4194304 | tf_op jit(solution)/shard_map/all_to_all | solution.py:183
  258.5 395.4 %all-gather.5.cloned.1.call-start = ((), (), s32[]{:S(2)}) async-start(), calls=%async_computation.6 | async-start | bytes 4259840 | tf_op jit(solution)/shard_map/all_gather | solution.py:188
  528.7 1.3 copy-start.1
  530.0 120.4 %all-to-all-start.2 = ((f32[4,128,2048]{2,1,0:T(8,128)}), f32[4,128,2048]{2,1,0:T(8,128)}, u32[]{:S(2)}, u32[]{:S(2)}) async-start(f32[4,128,2048]{2,1,0:T(8,128)} %bitcast.238), calls=%async_computation.3 | async-start | bytes 8388608 | tf_op jit(solution)/shard_map/all_to_all | solution.py:20
  553.4 3.3 copy-start.3
Sparse Core Ops, SparseCore 0:
  12.1 113.0 all-gather.2
  179.7 340.4 reduce-scatter.1
  524.1 114.6 all-gather.4
